TPU v7x, 32 devices: a whole 2x2x4 slice. The times are simulated.
32 devices in a mesh: dp: 16 (over z, y, core), inner: 2 (over x).
Axes of the slice: x: 2, y: 2, z: 4, core: 2. Of those that a mesh axis runs over, the one named last changes fastest.
Arguments:
- inputs: bfloat16 [32, 32, 32, 256], P(('dp', 'inner')), may hold values from -24 to 24
- cotangent: bfloat16 [32, 32, 32, 256], P(('dp', 'inner')), may hold values from -24 to 24
- kernel_taps: float32 [9, 256, 256], P(None, 'dp', 'inner'), may hold values from -1 to 1
Outputs:
- new_taps: float32 [9, 256, 256], P(None, 'dp', 'inner')
All inputs are finite; a program needn't handle non-finite values.
Results may differ from a plain program's by a relative error of at most 0.0003.
Values sent between devices are 32-bit elements; how exact they have to be, the bound alone decides.
No kernel may reach another device: no remote copies, remote signals or barrier semaphores. Data moves between devices by JAX's collectives and lax.ppermute only.
A program may use at most 64 MiB of HBM per device.

v0:
```python
import math
import jax
import jax.numpy as jnp
from jax import lax
from jax.sharding import PartitionSpec as P

MAPSIDE = 32
FREQS = 544
step_share = 0.06


def matmul(left_side, right_side):
    return jnp.dot(
        left_side, right_side, precision=lax.Precision.HIGHEST, preferred_element_type=jnp.float32
    )


def gradient_terms(inputs, cotangent):
    channels = inputs.shape[3]
    flat_cotangent = cotangent.reshape(-1, channels)
    collected = []
    for tap_index in range(9):
        row_off = tap_index // 3 - 1
        col_off = tap_index % 3 - 1
        shifted = jnp.roll(inputs, (-row_off, -col_off), axis=(1, 2))
        collected.append(
            lax.dot_general(
                shifted.reshape(-1, channels),
                flat_cotangent,
                (((0,), (0,)), ((), ())),
                preferred_element_type=jnp.float32,
            )
        )
    return jnp.stack(collected)


def phase_tables(freq_index, mapside, freq_count):
    row_shift = jnp.array([-1, -1, -1, 0, 0, 0, 1, 1, 1], dtype=jnp.int32)
    col_shift = jnp.array([-1, 0, 1, -1, 0, 1, -1, 0, 1], dtype=jnp.int32)
    half_width = mapside // 2 + 1
    first_freq = freq_index // half_width
    second_freq = freq_index % half_width
    turn_count = (
        first_freq[:, None] * row_shift[None, :] + second_freq[:, None] * col_shift[None, :]
    ) % mapside
    phase_angle = turn_count.astype(jnp.float32) * (2.0 * math.pi / mapside)
    live_mask = (freq_index < freq_count).astype(jnp.float32)[:, None]
    return (jnp.cos(phase_angle) * live_mask, jnp.sin(phase_angle) * live_mask)


def inverse_tables(freq_index, mapside, freq_count):
    cos_table, sin_table = phase_tables(freq_index, mapside, freq_count)
    second_freq = freq_index % (mapside // 2 + 1)
    on_edge = (second_freq == 0) | (second_freq == mapside // 2)
    weight = jnp.where(on_edge, 1.0, 2.0).astype(jnp.float32) / (mapside * mapside)
    return (cos_table * weight[:, None], sin_table * weight[:, None])


def bjorck(real_part, imag_part):
    matrix_size = real_part.shape[0]
    identity = jnp.eye(matrix_size, dtype=jnp.float32)
    for iteration in range(2):
        products = matmul(real_part.T, jnp.concatenate([real_part, imag_part], axis=1))
        square = matmul(imag_part.T, imag_part)
        cross_part = products[:, matrix_size:]
        gram_real = products[:, :matrix_size] + square
        gram_imag = cross_part - cross_part.T
        mix_real = 1.5 * identity - 0.5 * gram_real
        mix_imag = -0.5 * gram_imag
        stacked = jnp.concatenate(
            [
                jnp.concatenate([mix_real, mix_imag], axis=1),
                jnp.concatenate([-mix_imag, mix_real], axis=1),
            ],
            axis=0,
        )
        joined = matmul(jnp.concatenate([real_part, imag_part], axis=1), stacked)
        real_part, imag_part = (joined[:, :matrix_size], joined[:, matrix_size:])
    return (real_part, imag_part)


def orthonormalize(matrices):
    return bjorck(matrices[0], matrices[1])


def body(inputs, cotangent, kernel_taps):
    channels = inputs.shape[3]
    local_terms = gradient_terms(inputs, cotangent)
    partial_sum = lax.psum_scatter(local_terms, "dp", scatter_dimension=1, tiled=True)
    gradient = lax.psum_scatter(partial_sum, "inner", scatter_dimension=2, tiled=True)
    square_sum = lax.psum(jnp.sum(gradient * gradient), ("dp", "inner"))
    step_factor = step_share * math.sqrt(channels) / (jnp.sqrt(square_sum) + 1e-06)
    updated = kernel_taps - step_factor * gradient
    wide_count = lax.axis_size("dp")
    narrow = lax.axis_size("inner")
    freq_dev = -(-FREQS // (wide_count * narrow))
    in_rows = updated.shape[1]
    out_cols = updated.shape[2]
    col_blocks = lax.all_gather(updated, "inner", axis=2, tiled=True)
    gathered = lax.all_gather(col_blocks, "dp", axis=1, tiled=True)
    linear = lax.axis_index("dp") * narrow + lax.axis_index("inner")
    owned_freq = linear * freq_dev + jnp.arange(freq_dev, dtype=jnp.int32)
    cos_table, sin_table = phase_tables(owned_freq, MAPSIDE, FREQS)
    flattened = gathered.reshape(9, channels * channels)
    real_part = matmul(cos_table, flattened).reshape(freq_dev, channels, channels)
    imag_part = -matmul(sin_table, flattened).reshape(freq_dev, channels, channels)
    real_part, imag_part = lax.map(orthonormalize, (real_part, imag_part))
    returned = lax.all_to_all(
        lax.all_to_all(
            jnp.stack([real_part, imag_part], axis=1), "dp", split_axis=2, concat_axis=0, tiled=True
        ),
        "inner",
        split_axis=3,
        concat_axis=0,
        tiled=True,
    )
    slot_count = returned.shape[0]
    slot_index = jnp.arange(slot_count, dtype=jnp.int32)
    from_narrow = slot_index // (wide_count * freq_dev)
    from_wide = slot_index // freq_dev % wide_count
    freq_index = (from_wide * narrow + from_narrow) * freq_dev + slot_index % freq_dev
    weighted_cos, weighted_sin = inverse_tables(freq_index, MAPSIDE, FREQS)
    rebuilt = matmul(weighted_cos.T, returned[:, 0].reshape(slot_count, -1)) - matmul(
        weighted_sin.T, returned[:, 1].reshape(slot_count, -1)
    )
    return (math.sqrt(channels) * rebuilt).reshape(9, in_rows, out_cols)


def solution(mesh):
    placed = (
        P(("dp", "inner"), None, None, None),
        P(("dp", "inner"), None, None, None),
        P(None, "dp", "inner"),
    )
    return jax.shard_map(
        body, mesh=mesh, in_specs=placed, out_specs=P(None, "dp", "inner"), check_vma=False
    )
```

profile of v0, /device:TPU:0, one launch (start us, length us, event | category | flops | bytes accessed | tf_op | source)
XLA Modules:
  0.0 771.6 jit_solution(15128103214838415357)
XLA Ops:
  14.3 66.0 %reduce-scatter.3.cloned.1.call-done = f32[9,16,256]{2,1,0:T(8,128)} async-done(((f32[9,256,256]{2,1,0:T(8,128)}), f32[9,16,256]{2,1,0:T(8,128)}) %reduce-scatter.3.cloned.1.call-update) | async-done | bytes 147472 | tf_op jit(solution)/shard_map/reduce_scatter | solution.py:89
  80.4 11.6 %reduce-scatter.5.cloned.1.call-done = f32[9,16,128]{2,1,0:T(8,128)} async-done(((f32[9,16,256]{2,1,0:T(8,128)}), f32[9,16,128]{2,1,0:T(8,128)}) %reduce-scatter.5.cloned.1.call-update) | async-done | bytes 73744 | tf_op jit(solution)/shard_map/reduce_scatter | solution.py:90
  93.6 39.5 %psum.7 = f32[]{:T(128)} all-reduce(f32[]{:T(128)} %multiply_reduce_fusion), channel_id=1, replica_groups=mesh['dp'=16,'inner'=2] {'dp','inner'}, use_global_device_ids=true, to_apply=%region_3.4 | all-reduce | flops 1 | bytes 8 | tf_op jit(solution)/shard_map/psum | solution.py:91
  134.7 5.4 all_gather.6
  140.1 43.1 %all-gather.2.cloned.1.call-done = f32[9,256,256]{2,1,0:T(8,128)} async-done(((f32[9,16,256]{2,1,0:T(8,128)}), f32[9,256,256]{2,1,0:T(8,128)}) %all-gather.2.cloned.1.call-update) | async-done | bytes 2359312 | tf_op jit(solution)/shard_map/all_gather | solution.py:100
  185.2 8.6 %fusion.41 = f32[17,256,256]{2,0,1:T(8,128)} fusion(f32[256,256,9]{1,0,2:T(8,128)S(1)} %slice_bitcast_fusion.2, f32[17]{0:T(128)S(1)} %compare_convert_fusion.1, s32[9]{0:T(128)S(1)} %copy-done.6, s32[17]{0:T(128)S(1)} %get-tuple-element.110, s32[9]{0:T(128)S(1)} %copy-done.5, s32[17]{0:T(128)S(1)} %get-tuple-element.111), kind=kOutput, calls=%fused_computation.54 | convolution fusion | flops 121440808 | bytes 6816020 | tf_op jit(solution)/shard_map/dot_general | solution.py:13
  193.8 8.6 %fusion.33 = f32[17,256,256]{2,0,1:T(8,128)} fusion(f32[256,256,9]{1,0,2:T(8,128)S(1)} %slice_bitcast_fusion.2, f32[17]{0:T(128)S(1)} %compare_convert_fusion.1, s32[9]{0:T(128)S(1)} %copy-done.6, s32[17]{0:T(128)S(1)} %get-tuple-element.110, s32[9]{0:T(128)S(1)} %copy-done.5, s32[17]{0:T(128)S(1)} %get-tuple-element.111), kind=kOutput, calls=%fused_computation.46 | convolution fusion | flops 120326696 | bytes 6816020 | tf_op jit(solution)/shard_map/dot_general | solution.py:13
  202.4 145.4 %while.12 = (s32[]{:T(128)}, f32[17,256,256]{2,1,0:T(8,128)}, f32[17,256,256]{2,1,0:T(8,128)}, f32[17,256,256]{2,0,1:T(8,128)}, f32[17,256,256]{2,0,1:T(8,128)}, /*index=5*/s32[]{:T(128)}) while((s32[]{:T(128)}, f32[17,256,256]{2,1,0:T(8,128)}, f32[17,256,256]{2,1,0:T(8,128)}, f32[17,256,256]{2,0,1:T(8,128)}, f32[17,256,256]{2,0,1:T(8,128)}, ...), condition=%wide.region_5.6_spmd, body=%wide.region_4.5_spmd.sunk | while | flops 2821455872 | bytes 14942793 | solution.py:107
  202.4 2.6 constant_dynamic-slice_fusion.3
  210.9 2.6 constant_dynamic-slice_fusion.3
  219.5 2.6 constant_dynamic-slice_fusion.3
  228.1 2.6 constant_dynamic-slice_fusion.3
  236.6 2.6 constant_dynamic-slice_fusion.3
  245.2 2.6 constant_dynamic-slice_fusion.3
  253.7 2.6 constant_dynamic-slice_fusion.3
  262.3 2.6 constant_dynamic-slice_fusion.3
  279.4 2.6 constant_dynamic-slice_fusion.3
  288.0 2.6 constant_dynamic-slice_fusion.3
  313.6 2.6 constant_dynamic-slice_fusion.3
  322.2 2.6 constant_dynamic-slice_fusion.3
  339.2 2.6 constant_dynamic-slice_fusion.3
  347.8 4.6 pad_maximum_fusion.3
  352.4 23.6 %copy.89 = f32[17,2,256,256]{3,1,0,2:T(2,128)S(1)} copy(f32[17,2,256,256]{3,2,0,1:T(8,128)S(1)} %pad_maximum_fusion.3) | data formatting | bytes 17825792 | tf_op jit(solution)/shard_map/stack | solution.py:110
  376.0 196.4 %all_to_all.36 = f32[17,2,256,256]{3,1,0,2:T(2,128)S(1)} all-to-all(f32[17,2,256,256]{3,1,0,2:T(2,128)S(1)} %copy.89), channel_id=1, replica_groups=mesh['dp'=16,'inner'=2] {'dp'}, dimensions={2} | all-to-all | bytes 17825792 | tf_op jit(solution)/shard_map/all_to_all | solution.py:109
  573.7 4.5 copy.91
  578.2 11.6 %copy.92 = f32[272,2,16,256]{0,2,1,3:T(8,128)} copy(f32[272,2,16,256]{3,2,1,0:T(8,128)} %bitcast.179) | data formatting | bytes 17825792 | tf_op jit(solution)/shard_map/all_to_all | solution.py:109
  589.8 8.4 %all-to-all-start.1 = ((f32[272,2,16,256]{0,2,1,3:T(8,128)}), f32[272,2,16,256]{0,2,1,3:T(8,128)}, u32[]{:S(2)}, u32[]{:S(2)}) async-start(f32[272,2,16,256]{0,2,1,3:T(8,128)} %copy.92), calls=%async_computation.3 | async-start | bytes 25165824 | tf_op jit(solution)/shard_map/all_to_all | solution.py:108
  598.3 138.6 %all-to-all-done.1 = f32[272,2,16,256]{0,2,1,3:T(8,128)} async-done(((f32[272,2,16,256]{0,2,1,3:T(8,128)}), f32[272,2,16,256]{0,2,1,3:T(8,128)}, u32[]{:S(2)}, u32[]{:S(2)}) %all-to-all-start.1) | async-done | bytes 8912928 | tf_op jit(solution)/shard_map/all_to_all | solution.py:108
  736.8 14.6 %copy.97 = f32[272,2,16,2,128]{4,3,2,1,0:T(2,128)} copy(f32[272,2,16,2,128]{0,2,1,4,3:T(8,128)} %bitcast.42) | data formatting | bytes 17825792 | tf_op jit(solution)/shard_map/all_to_all | solution.py:108
  751.4 4.8 copy.94
  756.9 3.7 fusion.35
  760.7 3.7 fusion.47
  (308 shorter events, 124.4 us)
Async XLA Ops:
  6.5 2.9 copy-start
  6.5 2.6 copy-start.2
  6.5 73.8 %reduce-scatter.3.cloned.1.call-start = ((), (), s32[]{:S(2)}) async-start(), calls=%async_computation.4 | async-start | bytes 2506752 | tf_op jit(solution)/shard_map/reduce_scatter | solution.py:89
  12.1 121.7 %copy-start.4 = (f32[9,16,128]{2,1,0:T(8,128)S(1)}, f32[9,16,128]{2,1,0:T(8,128)}, u32[]{:S(2)}) copy-start(f32[9,16,128]{2,1,0:T(8,128)} %param.11) | copy-start | bytes 221188
  12.8 1.4 copy-start.3
  12.9 172.3 %copy-start.5 = (s32[9]{0:T(128)S(1)}, s32[9]{0:T(128)}, u32[]{:S(2)}) copy-start(s32[9]{0:T(128)} %constant.139.clone) | copy-start | bytes 112
  12.9 172.3 %copy-start.6 = (s32[9]{0:T(128)S(1)}, s32[9]{0:T(128)}, u32[]{:S(2)}) copy-start(s32[9]{0:T(128)} %constant.140.clone) | copy-start | bytes 112
  14.3 77.8 %reduce-scatter.5.cloned.1.call-start = ((), (), s32[]{:S(2)}) async-start(), calls=%async_computation.5 | async-start | bytes 221184 | tf_op jit(solution)/shard_map/reduce_scatter | solution.py:90
  80.4 102.9 %all-gather.2.cloned.1.call-start = ((), (), s32[]{:S(2)}) async-start(), calls=%async_computation.6 | async-start | bytes 2506752 | tf_op jit(solution)/shard_map/all_gather | solution.py:100
  589.8 147.1 %all-to-all-start.1 = ((f32[272,2,16,256]{0,2,1,3:T(8,128)}), f32[272,2,16,256]{0,2,1,3:T(8,128)}, u32[]{:S(2)}, u32[]{:S(2)}) async-start(f32[272,2,16,256]{0,2,1,3:T(8,128)} %copy.92), calls=%async_computation.3 | async-start | bytes 25165824 | tf_op jit(solution)/shard_map/all_to_all | solution.py:108
  756.9 8.2 %copy-start.1 = (bf16[1,32,32,256]{3,2,1,0:T(8,128)(2,1)S(1)}, bf16[1,32,32,256]{3,2,1,0:T(8,128)(2,1)}, u32[]{:S(2)}) copy-start(bf16[1,32,32,256]{3,2,1,0:T(8,128)(2,1)} %param.10) | copy-start | bytes 1572868
Sparse Core Ops, SparseCore 0:
  14.4 65.9 reduce-scatter.2
  82.6 9.4 reduce-scatter.4
  140.2 43.0 all-gather.1
where the time goes:
time: 773 us; the launch traced here: 772 us
  waiting for transfers between devices  259 us (34%)
  blocking collectives  241 us (31%)
  local copies, waits for them, and re-layouts  132 us (17%)
  matrix products  105 us (14%)
  between operations  14.1 us (2%)
  other arithmetic  9.14 us (1%)
  starting transfers between devices  8.48 us (1%)
    all_to_all x1, blocking collectives, body(): lax.all_to_all(jnp.stack([real_part, imag_part], axis=1), 'dp', split_axi...  196 us
    all_to_all x1, waiting for transfers between devices, body(): lax.all_to_all(lax.all_to_all(jnp.stack([real_part, imag_part], axis=1),...  139 us
    dot_general x106, matrix products, matmul(): jnp.dot(left_side, right_side, precision=lax.Precision.HIGHEST, preferred...  102 us
    reduce_scatter x1, waiting for transfers between devices, body(): lax.psum_scatter(local_terms, 'dp', scatter_dimension=1, tiled=True)  66 us
    dynamic_slice x51, local copies, waits for them, and re-layouts, body(): real_part, imag_part = lax.map(orthonormalize, (real_part, imag_part))  44.9 us
    all_gather x1, waiting for transfers between devices, body(): gathered = lax.all_gather(col_blocks, 'dp', axis=1, tiled=True)  43.1 us
    psum x1, blocking collectives, body(): square_sum = lax.psum(jnp.sum(gradient * gradient), ('dp', 'inner'))  39.5 us
    another operation x1, local copies, waits for them, and re-layouts, body(): jnp.stack([real_part, imag_part], axis=1)  23.6 us
  transfers between devices with their start and end apart: 4, of which 4 were waited for; matrix products, arithmetic and copies ran while one was open for 0% of the time, Pallas kernels for 0%

commit v1 on v0

--- a/solution.py
+++ b/solution.py
@@ -105,15 +105,12 @@
     real_part = matmul(cos_table, flattened).reshape(freq_dev, channels, channels)
     imag_part = -matmul(sin_table, flattened).reshape(freq_dev, channels, channels)
     real_part, imag_part = lax.map(orthonormalize, (real_part, imag_part))
-    returned = lax.all_to_all(
-        lax.all_to_all(
-            jnp.stack([real_part, imag_part], axis=1), "dp", split_axis=2, concat_axis=0, tiled=True
-        ),
-        "inner",
-        split_axis=3,
-        concat_axis=0,
-        tiled=True,
+    block = lax.all_to_all(
+        jnp.stack([real_part, imag_part], axis=1), "dp", split_axis=2, concat_axis=0, tiled=True
     )
+    cells = jnp.split(block, lax.axis_size("inner"), axis=3)
+    got = lax.all_to_all(jnp.stack(cells), "inner", 0, 0)
+    returned = jnp.concatenate(got, axis=0)
     slot_count = returned.shape[0]
     slot_index = jnp.arange(slot_count, dtype=jnp.int32)
     from_narrow = slot_index // (wide_count * freq_dev)

time: 773 us -> 707 us (0.915)
  waiting for transfers between devices: 259 us -> 220 us
  local copies, waits for them, and re-layouts: 132 us -> 103 us
    all_to_all x1, waiting for transfers between devices: 139 us -> 99 us  [body(): got = lax.all_to_all(jnp.stack(cells), 'inner', 0, 0)]
    all_to_all x2 -> x0, local copies, waits for them, and re-layouts: 19.4 us -> none  [body(): lax.all_to_all(lax.all_to_all(jnp.stack([real_part, imag_part], axis=1),...]
    all_to_all x3 -> x2, local copies, waits for them, and re-layouts: 17.3 us -> 2.79 us  [body(): lax.all_to_all(jnp.stack([real_part, imag_part], axis=1), 'dp', split_axi...]
where the time goes in v1:
time: 707 us; the launch traced here: 706 us
  blocking collectives  241 us (34%)
  waiting for transfers between devices  220 us (31%)
  matrix products  105 us (15%)
  local copies, waits for them, and re-layouts  103 us (15%)
  between operations  14.1 us (2%)
  other arithmetic  13.7 us (2%)
  starting transfers between devices  7.44 us (1%)
    all_to_all x1, blocking collectives, body(): lax.all_to_all(jnp.stack([real_part, imag_part], axis=1), 'dp', split_axi...  196 us
    dot_general x106, matrix products, matmul(): jnp.dot(left_side, right_side, precision=lax.Precision.HIGHEST, preferred...  102 us
    all_to_all x1, waiting for transfers between devices, body(): got = lax.all_to_all(jnp.stack(cells), 'inner', 0, 0)  99 us
    reduce_scatter x1, waiting for transfers between devices, body(): lax.psum_scatter(local_terms, 'dp', scatter_dimension=1, tiled=True)  66 us
    dynamic_slice x51, local copies, waits for them, and re-layouts, body(): real_part, imag_part = lax.map(orthonormalize, (real_part, imag_part))  44.9 us
    all_gather x1, waiting for transfers between devices, body(): gathered = lax.all_gather(col_blocks, 'dp', axis=1, tiled=True)  43.1 us
    psum x1, blocking collectives, body(): square_sum = lax.psum(jnp.sum(gradient * gradient), ('dp', 'inner'))  39.5 us
    another operation x1, local copies, waits for them, and re-layouts, body(): jnp.stack([real_part, imag_part], axis=1)  23.6 us
  transfers between devices with their start and end apart: 4, of which 4 were waited for; matrix products, arithmetic and copies ran while one was open for 0% of the time, Pallas kernels for 0%

profile of v1, /device:TPU:0, one launch (start us, length us, event | category | flops | bytes accessed | tf_op | source)
XLA Modules:
  0.0 706.4 jit_solution(18281122261173701510)
XLA Ops:
  14.4 66.0 %reduce-scatter.3.cloned.1.call-done = f32[9,16,256]{2,1,0:T(8,128)} async-done(((f32[9,256,256]{2,1,0:T(8,128)}), f32[9,16,256]{2,1,0:T(8,128)}) %reduce-scatter.3.cloned.1.call-update) | async-done | bytes 147472 | tf_op jit(solution)/shard_map/reduce_scatter | solution.py:89
  80.5 11.6 %reduce-scatter.5.cloned.1.call-done = f32[9,16,128]{2,1,0:T(8,128)} async-done(((f32[9,16,256]{2,1,0:T(8,128)}), f32[9,16,128]{2,1,0:T(8,128)}) %reduce-scatter.5.cloned.1.call-update) | async-done | bytes 73744 | tf_op jit(solution)/shard_map/reduce_scatter | solution.py:90
  93.6 39.5 %psum.7 = f32[]{:T(128)} all-reduce(f32[]{:T(128)} %multiply_reduce_fusion), channel_id=1, replica_groups=mesh['dp'=16,'inner'=2] {'dp','inner'}, use_global_device_ids=true, to_apply=%region_3.4 | all-reduce | flops 1 | bytes 8 | tf_op jit(solution)/shard_map/psum | solution.py:91
  134.7 5.4 all_gather.6
  140.2 43.1 %all-gather.2.cloned.1.call-done = f32[9,256,256]{2,1,0:T(8,128)} async-done(((f32[9,16,256]{2,1,0:T(8,128)}), f32[9,256,256]{2,1,0:T(8,128)}) %all-gather.2.cloned.1.call-update) | async-done | bytes 2359312 | tf_op jit(solution)/shard_map/all_gather | solution.py:100
  185.2 8.6 %fusion.41 = f32[17,256,256]{2,0,1:T(8,128)} fusion(f32[256,256,9]{1,0,2:T(8,128)S(1)} %slice_bitcast_fusion.4, f32[17]{0:T(128)S(1)} %compare_convert_fusion.1, s32[9]{0:T(128)S(1)} %copy-done.6, s32[17]{0:T(128)S(1)} %get-tuple-element.107, s32[9]{0:T(128)S(1)} %copy-done.5, s32[17]{0:T(128)S(1)} %get-tuple-element.108), kind=kOutput, calls=%fused_computation.57 | convolution fusion | flops 121440808 | bytes 6816020 | tf_op jit(solution)/shard_map/dot_general | solution.py:13
  193.8 8.6 %fusion.33 = f32[17,256,256]{2,0,1:T(8,128)} fusion(f32[256,256,9]{1,0,2:T(8,128)S(1)} %slice_bitcast_fusion.4, f32[17]{0:T(128)S(1)} %compare_convert_fusion.1, s32[9]{0:T(128)S(1)} %copy-done.6, s32[17]{0:T(128)S(1)} %get-tuple-element.107, s32[9]{0:T(128)S(1)} %copy-done.5, s32[17]{0:T(128)S(1)} %get-tuple-element.108), kind=kOutput, calls=%fused_computation.47 | convolution fusion | flops 120326696 | bytes 6816020 | tf_op jit(solution)/shard_map/dot_general | solution.py:13
  202.4 145.3 %while.12 = (s32[]{:T(128)}, f32[17,256,256]{2,1,0:T(8,128)}, f32[17,256,256]{2,1,0:T(8,128)}, f32[17,256,256]{2,0,1:T(8,128)}, f32[17,256,256]{2,0,1:T(8,128)}, /*index=5*/s32[]{:T(128)}) while((s32[]{:T(128)}, f32[17,256,256]{2,1,0:T(8,128)}, f32[17,256,256]{2,1,0:T(8,128)}, f32[17,256,256]{2,0,1:T(8,128)}, f32[17,256,256]{2,0,1:T(8,128)}, ...), condition=%wide.region_5.6_spmd, body=%wide.region_4.5_spmd.sunk | while | flops 2821455872 | bytes 14942793 | solution.py:107
  202.4 2.6 constant_dynamic-slice_fusion.3
  211.0 2.6 constant_dynamic-slice_fusion.3
  219.5 2.6 constant_dynamic-slice_fusion.3
  228.1 2.6 constant_dynamic-slice_fusion.3
  236.6 2.6 constant_dynamic-slice_fusion.3
  245.2 2.6 constant_dynamic-slice_fusion.3
  253.7 2.6 constant_dynamic-slice_fusion.3
  262.2 2.6 constant_dynamic-slice_fusion.3
  270.8 2.6 constant_dynamic-slice_fusion.3
  279.3 2.6 constant_dynamic-slice_fusion.3
  287.9 2.6 constant_dynamic-slice_fusion.3
  296.4 2.6 constant_dynamic-slice_fusion.3
  305.0 2.6 constant_dynamic-slice_fusion.3
  313.5 2.6 constant_dynamic-slice_fusion.3
  322.0 2.6 constant_dynamic-slice_fusion.3
  347.7 4.6 pad_maximum_fusion.3
  352.3 23.6 %copy.68 = f32[17,2,256,256]{3,1,0,2:T(2,128)S(1)} copy(f32[17,2,256,256]{3,2,0,1:T(8,128)S(1)} %pad_maximum_fusion.3) | data formatting | bytes 17825792 | tf_op jit(solution)/shard_map/stack | solution.py:109
  375.9 196.5 %all_to_all.23 = f32[17,2,256,256]{3,1,0,2:T(2,128)S(1)} all-to-all(f32[17,2,256,256]{3,1,0,2:T(2,128)S(1)} %copy.68), channel_id=1, replica_groups=mesh['dp'=16,'inner'=2] {'dp'}, dimensions={2} | all-to-all | bytes 17825792 | tf_op jit(solution)/shard_map/all_to_all | solution.py:108
  576.4 4.5 pad_maximum_fusion.4
  580.9 7.4 %all-to-all-start.1 = ((f32[2,272,2,16,128]{4,3,2,1,0:T(8,128)}), f32[2,272,2,16,128]{4,3,2,1,0:T(8,128)}, u32[]{:S(2)}, u32[]{:S(2)}) async-start(f32[2,272,2,16,128]{4,3,2,1,0:T(8,128)} %pad_maximum_fusion.4), calls=%async_computation.3 | async-start | bytes 17825792 | tf_op jit(solution)/shard_map/all_to_all | solution.py:112
  588.4 99.0 %all-to-all-done.1 = f32[2,272,2,16,128]{4,3,2,1,0:T(8,128)} async-done(((f32[2,272,2,16,128]{4,3,2,1,0:T(8,128)}), f32[2,272,2,16,128]{4,3,2,1,0:T(8,128)}, u32[]{:S(2)}, u32[]{:S(2)}) %all-to-all-start.1) | async-done | bytes 8912928 | tf_op jit(solution)/shard_map/all_to_all | solution.py:112
  687.4 4.2 fusion.199
  691.7 3.7 fusion.35
  695.4 3.7 fusion.47
  (307 shorter events, 121.2 us)
Async XLA Ops:
  6.5 2.9 copy-start
  6.5 2.6 copy-start.2
  6.5 73.8 %reduce-scatter.3.cloned.1.call-start = ((), (), s32[]{:S(2)}) async-start(), calls=%async_computation.4 | async-start | bytes 2506752 | tf_op jit(solution)/shard_map/reduce_scatter | solution.py:89
  12.1 121.7 %copy-start.4 = (f32[9,16,128]{2,1,0:T(8,128)S(1)}, f32[9,16,128]{2,1,0:T(8,128)}, u32[]{:S(2)}) copy-start(f32[9,16,128]{2,1,0:T(8,128)} %param.11) | copy-start | bytes 221188
  12.8 1.4 copy-start.3
  12.9 172.3 %copy-start.5 = (s32[9]{0:T(128)S(1)}, s32[9]{0:T(128)}, u32[]{:S(2)}) copy-start(s32[9]{0:T(128)} %constant.139.clone) | copy-start | bytes 112
  12.9 172.3 %copy-start.6 = (s32[9]{0:T(128)S(1)}, s32[9]{0:T(128)}, u32[]{:S(2)}) copy-start(s32[9]{0:T(128)} %constant.140.clone) | copy-start | bytes 112
  14.3 77.8 %reduce-scatter.5.cloned.1.call-start = ((), (), s32[]{:S(2)}) async-start(), calls=%async_computation.5 | async-start | bytes 221184 | tf_op jit(solution)/shard_map/reduce_scatter | solution.py:90
  80.4 102.9 %all-gather.2.cloned.1.call-start = ((), (), s32[]{:S(2)}) async-start(), calls=%async_computation.6 | async-start | bytes 2506752 | tf_op jit(solution)/shard_map/all_gather | solution.py:100
  580.9 106.5 %all-to-all-start.1 = ((f32[2,272,2,16,128]{4,3,2,1,0:T(8,128)}), f32[2,272,2,16,128]{4,3,2,1,0:T(8,128)}, u32[]{:S(2)}, u32[]{:S(2)}) async-start(f32[2,272,2,16,128]{4,3,2,1,0:T(8,128)} %pad_maximum_fusion.4), calls=%async_computation.3 | async-start | bytes 17825792 | tf_op jit(solution)/shard_map/all_to_all | solution.py:112
  691.7 8.2 %copy-start.1 = (bf16[1,32,32,256]{3,2,1,0:T(8,128)(2,1)S(1)}, bf16[1,32,32,256]{3,2,1,0:T(8,128)(2,1)}, u32[]{:S(2)}) copy-start(bf16[1,32,32,256]{3,2,1,0:T(8,128)(2,1)} %param.10) | copy-start | bytes 1572868
Sparse Core Ops, SparseCore 0:
  14.4 65.9 reduce-scatter.2
  82.6 9.4 reduce-scatter.4
  140.2 43.0 all-gather.1
